TPU v7x, 256 devices: a whole 4x4x8 slice. The times are simulated.
256 devices in a mesh: row: 32 (over z, y), col: 8 (over x, core).
Axes of the slice: x: 4, y: 4, z: 8, core: 2. Of those that a mesh axis runs over, the one named last changes fastest.
Arguments:
- inputs: bfloat16 [16384, 2048], P('row', 'col'), may hold values from -6 to 6
- grad_out: bfloat16 [16384, 2048], P('row', 'col'), may hold values from -6 to 6
- gate_pre: bfloat16 [16384, 7168], P('row', 'col'), may hold values from -8 to 8
- up_pre: bfloat16 [16384, 7168], P('row', 'col'), may hold values from -6 to 6
- gate_weight: bfloat16 [2048, 7168], P('row', 'col'), may hold values from -0.125 to 0.125
- up_weight: bfloat16 [2048, 7168], P('row', 'col'), may hold values from -0.125 to 0.125
- down_weight: bfloat16 [2048, 7168], P('row', 'col'), may hold values from -0.125 to 0.125
Outputs:
- d_inputs: bfloat16 [16384, 2048], P('row', 'col')
- gate_grad: bfloat16 [2048, 7168], P('row', 'col')
- up_grad: bfloat16 [2048, 7168], P('row', 'col')
- down_grad: bfloat16 [2048, 7168], P('row', 'col')
All inputs are finite; a program needn't handle non-finite values.
Results may differ from a plain program's by a relative error of at most 0.015.
Values may be sent and summed in bfloat16 or wider, within the bound.
No kernel may reach another device: no remote copies, remote signals or barrier semaphores. Data moves between devices by JAX's collectives and lax.ppermute only.
A program may use at most 128 MiB of HBM per device.

v0:
```python
import math
import jax
import jax.numpy as jnp
from jax import lax
from jax.sharding import PartitionSpec as P


def against(left, right):
    return lax.dot_general(
        left, right, (((1,), (1,)), ((), ())), preferred_element_type=jnp.float32
    )


def body(inputs, grad_out, gate_pre, up_pre, gate_weight, up_weight, down_weight):
    rows_here = grad_out.shape[0]
    hidden_here = gate_pre.shape[1]
    factor = 1.0 / math.sqrt(rows_here * lax.axis_size("row"))
    full_inputs, full_grads = (
        lax.all_gather(inputs, "col", axis=1, tiled=True),
        lax.all_gather(grad_out, "col", axis=1, tiled=True),
    )
    d_hidden = jnp.dot(
        full_grads,
        lax.all_gather(down_weight, "row", axis=0, tiled=True),
        preferred_element_type=jnp.float32,
    )
    gate_vals = gate_pre.astype(jnp.float32)
    up_vals = up_pre.astype(jnp.float32)
    sigma = jax.nn.sigmoid(gate_vals)
    active = gate_vals * sigma
    hidden = (active * up_vals).astype(jnp.bfloat16)
    d_gate = (d_hidden * up_vals * sigma * (1.0 + gate_vals * (1.0 - sigma))).astype(jnp.bfloat16)
    d_up = (d_hidden * active).astype(jnp.bfloat16)

    def grad_term(left, right):
        product = lax.dot_general(
            left, right, (((0,), (0,)), ((), ())), preferred_element_type=jnp.float32
        )
        return product * factor

    down_grad = lax.psum_scatter(
        grad_term(full_grads, hidden).astype(jnp.bfloat16), "row", scatter_dimension=0, tiled=True
    )
    part = against(d_gate, lax.all_gather(gate_weight, "row", axis=0, tiled=True)) + against(
        d_up, lax.all_gather(up_weight, "row", axis=0, tiled=True)
    )
    d_inputs = lax.psum_scatter(part.astype(jnp.bfloat16), "col", scatter_dimension=1, tiled=True)
    paired = lax.psum_scatter(
        jnp.concatenate(
            [grad_term(full_inputs, d_gate), grad_term(full_inputs, d_up)], axis=1
        ).astype(jnp.bfloat16),
        "row",
        scatter_dimension=0,
        tiled=True,
    ).astype(jnp.float32)
    gate_grad = paired[:, :hidden_here].astype(jnp.bfloat16)
    up_grad = paired[:, hidden_here:].astype(jnp.bfloat16)
    return (d_inputs, gate_grad, up_grad, down_grad)


def solution(mesh):
    in_specs = (
        P("row", "col"),
        P("row", "col"),
        P("row", "col"),
        P("row", "col"),
        P("row", "col"),
        P("row", "col"),
        P("row", "col"),
    )
    out_specs = (P("row", "col"), P("row", "col"), P("row", "col"), P("row", "col"))
    return jax.shard_map(body, mesh=mesh, in_specs=in_specs, out_specs=out_specs, check_vma=False)
```

profile of v0, /device:TPU:8, one launch (start us, length us, event | category | flops | bytes accessed | tf_op | source)
XLA Modules:
  0.0 815.9 jit_solution(1968349745473048420)
XLA Ops:
  7.2 0.7 all-gather.6.cloned.1.call-update
  7.9 0.7 all-gather.8.cloned.1.call-update
  8.7 0.7 all-gather.14.cloned.1.call-update
  9.4 0.5 all-gather.10.cloned.1.call-update
  10.0 0.5 all-gather.12.cloned.1.call-update
  10.6 31.4 %all-gather.6.cloned.1.call-done = bf16[512,2048]{1,0:T(8,128)(2,1)} async-done(((bf16[512,256]{1,0:T(8,128)(2,1)}), bf16[512,2048]{1,0:T(8,128)(2,1)}) %all-gather.6.cloned.1.call-update) | async-done | bytes 2097168 | tf_op jit(solution)/shard_map/all_gather | solution.py:20
  42.0 83.0 %all-gather.8.cloned.1.call-done = bf16[2048,896]{1,0:T(8,128)(2,1)} async-done(((bf16[64,896]{1,0:T(8,128)(2,1)}), bf16[2048,896]{1,0:T(8,128)(2,1)}) %all-gather.8.cloned.1.call-update) | async-done | bytes 3670032 | tf_op jit(solution)/shard_map/all_gather | solution.py:24
  125.0 7.0 fusion.5
  132.0 22.2 %all-gather.14.cloned.1.call-done = bf16[512,2048]{1,0:T(8,128)(2,1)} async-done(((bf16[512,256]{1,0:T(8,128)(2,1)}), bf16[512,2048]{1,0:T(8,128)(2,1)}) %all-gather.14.cloned.1.call-update) | async-done | bytes 2097168 | tf_op jit(solution)/shard_map/all_gather | solution.py:19
  154.2 3.8 fusion
  158.1 4.1 fusion.1
  162.2 6.2 pad_maximum_fusion
  168.4 10.1 %copy.17 = bf16[2048,1792]{1,0:T(8,128)(2,1)} copy(bf16[2048,1792]{0,1:T(8,128)(2,1)} %pad_maximum_fusion) | data formatting | bytes 14680064
  178.5 1.5 copy-done
  180.3 5.3 fusion.2
  185.6 6.1 copy.19
  191.9 45.1 %all-gather.10.cloned.1.call-done = bf16[2048,896]{1,0:T(8,128)(2,1)} async-done(((bf16[64,896]{1,0:T(8,128)(2,1)}), bf16[2048,896]{1,0:T(8,128)(2,1)}) %all-gather.10.cloned.1.call-update) | async-done | bytes 3670032 | tf_op jit(solution)/shard_map/all_gather | solution.py:44
  237.1 6.5 fusion.14
  243.5 73.4 %all-gather.12.cloned.1.call-done = bf16[2048,896]{1,0:T(8,128)(2,1)} async-done(((bf16[64,896]{1,0:T(8,128)(2,1)}), bf16[2048,896]{1,0:T(8,128)(2,1)}) %all-gather.12.cloned.1.call-update) | async-done | bytes 3670032 | tf_op jit(solution)/shard_map/all_gather | solution.py:45
  317.0 7.6 add_convert_fusion
  324.5 221.4 %reduce-scatter.10.cloned.1.call-done = bf16[64,1792]{1,0:T(8,128)(2,1)} async-done(((bf16[2048,1792]{1,0:T(8,128)(2,1)}), bf16[64,1792]{1,0:T(8,128)(2,1)}) %reduce-scatter.10.cloned.1.call-update) | async-done | bytes 229392
  545.9 1.7 fusion.13
  547.6 222.8 %reduce-scatter.12.cloned.1.call-done = bf16[64,896]{1,0:T(8,128)(2,1)} async-done(((bf16[2048,896]{1,0:T(8,128)(2,1)}), bf16[64,896]{1,0:T(8,128)(2,1)}) %reduce-scatter.12.cloned.1.call-update) | async-done | bytes 114704
  770.4 38.6 %reduce-scatter.8.cloned.1.call-done = bf16[512,256]{1,0:T(8,128)(2,1)} async-done(((bf16[512,2048]{1,0:T(8,128)(2,1)}), bf16[512,256]{1,0:T(8,128)(2,1)}) %reduce-scatter.8.cloned.1.call-update) | async-done | bytes 262160 | tf_op jit(solution)/shard_map/reduce_scatter | solution.py:47
  (26 shorter events, 0.8 us)
Async XLA Ops:
  7.2 34.8 %all-gather.6.cloned.1.call-start = ((), (), s32[]{:S(2)}) async-start(), calls=%async_computation.3 | async-start | bytes 2359296 | tf_op jit(solution)/shard_map/all_gather | solution.py:20
  7.9 117.1 %all-gather.8.cloned.1.call-start = ((), (), s32[]{:S(2)}) async-start(), calls=%async_computation.4 | async-start | bytes 3784704 | tf_op jit(solution)/shard_map/all_gather | solution.py:24
  8.6 145.6 %all-gather.14.cloned.1.call-start = ((), (), s32[]{:S(2)}) async-start(), calls=%async_computation.8 | async-start | bytes 2359296 | tf_op jit(solution)/shard_map/all_gather | solution.py:19
  9.4 227.7 %all-gather.10.cloned.1.call-start = ((), (), s32[]{:S(2)}) async-start(), calls=%async_computation.5 | async-start | bytes 3784704 | tf_op jit(solution)/shard_map/all_gather | solution.py:44
  10.0 307.0 %all-gather.12.cloned.1.call-start = ((), (), s32[]{:S(2)}) async-start(), calls=%async_computation.6 | async-start | bytes 3784704 | tf_op jit(solution)/shard_map/all_gather | solution.py:45
  10.5 535.4 %reduce-scatter.10.cloned.1.call-start = ((), (), s32[]{:S(2)}) async-start(), calls=%async_computation.9 | async-start | bytes 7569408
  132.0 26.1 %copy-start.5 = (bf16[512,896]{1,0:T(8,128)(2,1)}, bf16[512,896]{1,0:T(8,128)(2,1)S(1)}, u32[]{:S(2)}) copy-start(bf16[512,896]{1,0:T(8,128)(2,1)S(1)} %get-tuple-element.14) | copy-start | bytes 2752516
  154.2 3.9 copy-start.1
  154.2 3.9 copy-start.3
  154.2 3.9 copy-start.7
  178.5 1.6 copy-start
  178.5 1.8 copy-start.2
  178.5 592.0 %reduce-scatter.12.cloned.1.call-start = ((), (), s32[]{:S(2)}) async-start(), calls=%async_computation.10 | async-start | bytes 3784704
  191.7 45.4 %copy-start.6 = (bf16[512,896]{1,0:T(8,128)(2,1)S(1)}, bf16[512,896]{1,0:T(8,128)(2,1)}, u32[]{:S(2)}) copy-start(bf16[512,896]{1,0:T(8,128)(2,1)} %copy-done.5) | copy-start | bytes 2752516
  191.7 125.3 %copy-start.4 = (bf16[512,896]{1,0:T(8,128)(2,1)S(1)}, bf16[512,896]{1,0:T(8,128)(2,1)}, u32[]{:S(2)}) copy-start(bf16[512,896]{1,0:T(8,128)(2,1)} %param.9) | copy-start | bytes 2752516
  191.7 617.4 %reduce-scatter.8.cloned.1.call-start = ((), (), s32[]{:S(2)}) async-start(), calls=%async_computation.7 | async-start | bytes 2359296 | tf_op jit(solution)/shard_map/reduce_scatter | solution.py:47
Sparse Core Ops, SparseCore 0:
  9.8 32.1 all-gather.5
  44.6 80.3 all-gather.7
  126.8 27.3 all-gather.13
  156.6 80.3 all-gather.9
  239.5 77.4 all-gather.11
  320.8 225.0 reduce-scatter.9
  550.4 220.0 reduce-scatter.11
  773.6 35.4 reduce-scatter.7
where the time goes:
time: 817 us; the launch traced here: 816 us
  waiting for transfers between devices  741 us (91%)
  matrix products  34.2 us (4%)
  local copies, waits for them, and re-layouts  19.6 us (2%)
  between operations  14.2 us (2%)
    unnamed x10, waiting for transfers between devices  447 us
    all_gather x1, waiting for transfers between devices, body(): lax.all_gather(down_weight, 'row', axis=0, tiled=True)  83 us
    all_gather x1, waiting for transfers between devices, body(): lax.all_gather(up_weight, 'row', axis=0, tiled=True)  73.4 us
    all_gather x1, waiting for transfers between devices, body(): lax.all_gather(gate_weight, 'row', axis=0, tiled=True)  45.1 us
    reduce_scatter x1, waiting for transfers between devices, body(): lax.psum_scatter(part.astype(jnp.bfloat16), 'col', scatter_dimension=1, t...  38.6 us
    all_gather x1, waiting for transfers between devices, body(): lax.all_gather(grad_out, 'col', axis=1, tiled=True)  31.4 us
    all_gather x1, waiting for transfers between devices, body(): lax.all_gather(inputs, 'col', axis=1, tiled=True)  22.2 us
    unnamed x18, local copies, waits for them, and re-layouts  17.9 us
  transfers between devices with their start and end apart: 8, of which 8 were waited for; matrix products, arithmetic and copies ran while one was open for 7% of the time, Pallas kernels for 0%

commit v1 on v0

--- a/solution.py
+++ b/solution.py
@@ -3,6 +3,11 @@
 import jax.numpy as jnp
 from jax import lax
 from jax.sharding import PartitionSpec as P
+
+
+def swapped_in(x, name, along):
+    outgoing = jnp.stack([x] * lax.axis_size(name))
+    return jnp.concatenate(lax.all_to_all(outgoing, name, 0, 0), axis=along)
 
 
 def against(left, right):
@@ -41,7 +46,7 @@
     down_grad = lax.psum_scatter(
         grad_term(full_grads, hidden).astype(jnp.bfloat16), "row", scatter_dimension=0, tiled=True
     )
-    part = against(d_gate, lax.all_gather(gate_weight, "row", axis=0, tiled=True)) + against(
+    part = against(d_gate, swapped_in(gate_weight, "row", 0)) + against(
         d_up, lax.all_gather(up_weight, "row", axis=0, tiled=True)
     )
     d_inputs = lax.psum_scatter(part.astype(jnp.bfloat16), "col", scatter_dimension=1, tiled=True)

time: 817 us -> 779 us (0.953)
  waiting for transfers between devices: 741 us -> 691 us
  starting transfers between devices: 0.49 us -> 10.9 us
    all_to_all x0 -> x1, waiting for transfers between devices: none -> 88 us  [swapped_in(): return jnp.concatenate(lax.all_to_all(outgoing, name, 0, 0), axis=along)]
    all_gather x1, waiting for transfers between devices: 73.4 us -> 0.01 us  [body(): lax.all_gather(up_weight, 'row', axis=0, tiled=True)]
    all_gather x1 -> x0, waiting for transfers between devices: 45.1 us -> none  [body(): lax.all_gather(gate_weight, 'row', axis=0, tiled=True)]
    unnamed x10 -> x9, waiting for transfers between devices: 447 us -> 428 us
    all_to_all x0 -> x1, starting transfers between devices: none -> 10.5 us  [swapped_in(): return jnp.concatenate(lax.all_to_all(outgoing, name, 0, 0), axis=along)]
    unnamed x18 -> x20, local copies, waits for them, and re-layouts: 17.9 us -> 17.1 us
  transfers between devices with their start and end apart: 8 -> 8, of which waited for: 8 -> 7; matrix products, arithmetic and copies ran while one was open for 7% -> 8% of each run, Pallas kernels for 0% -> 0%
where the time goes in v1:
time: 779 us; the launch traced here: 778 us
  waiting for transfers between devices  691 us (89%)
  matrix products  34.6 us (4%)
  local copies, waits for them, and re-layouts  21.2 us (3%)
  between operations  14.2 us (2%)
  starting transfers between devices  10.9 us (1%)
    unnamed x9, waiting for transfers between devices  428 us
    all_to_all x1, waiting for transfers between devices, swapped_in(): return jnp.concatenate(lax.all_to_all(outgoing, name, 0, 0), axis=along)  88 us
    all_gather x1, waiting for transfers between devices, body(): lax.all_gather(down_weight, 'row', axis=0, tiled=True)  83 us
    reduce_scatter x1, waiting for transfers between devices, body(): lax.psum_scatter(part.astype(jnp.bfloat16), 'col', scatter_dimension=1, t...  38.7 us
    all_gather x1, waiting for transfers between devices, body(): lax.all_gather(grad_out, 'col', axis=1, tiled=True)  32 us
    all_gather x1, waiting for transfers between devices, body(): lax.all_gather(inputs, 'col', axis=1, tiled=True)  22.2 us
    unnamed x20, local copies, waits for them, and re-layouts  17.1 us
  transfers between devices with their start and end apart: 8, of which 7 were waited for; matrix products, arithmetic and copies ran while one was open for 8% of the time, Pallas kernels for 0%

profile of v1, /device:TPU:8, one launch (start us, length us, event | category | flops | bytes accessed | tf_op | source)
XLA Modules:
  0.0 778.5 jit_solution(13302332286418441859)
XLA Ops:
  7.2 0.7 all-gather.5.cloned.1.call-update
  7.9 0.7 all-gather.7.cloned.1.call-update
  8.7 0.7 all-gather.11.cloned.1.call-update
  9.4 0.5 all-gather.9.cloned.1.call-update
  10.0 32.0 %all-gather.5.cloned.1.call-done = bf16[512,2048]{1,0:T(8,128)(2,1)} async-done(((bf16[512,256]{1,0:T(8,128)(2,1)}), bf16[512,2048]{1,0:T(8,128)(2,1)}) %all-gather.5.cloned.1.call-update) | async-done | bytes 2097168 | tf_op jit(solution)/shard_map/all_gather | solution.py:25
  42.0 83.0 %all-gather.7.cloned.1.call-done = bf16[2048,896]{1,0:T(8,128)(2,1)} async-done(((bf16[64,896]{1,0:T(8,128)(2,1)}), bf16[2048,896]{1,0:T(8,128)(2,1)}) %all-gather.7.cloned.1.call-update) | async-done | bytes 3670032 | tf_op jit(solution)/shard_map/all_gather | solution.py:29
  125.0 7.0 fusion.5
  132.0 22.2 %all-gather.11.cloned.1.call-done = bf16[512,2048]{1,0:T(8,128)(2,1)} async-done(((bf16[512,256]{1,0:T(8,128)(2,1)}), bf16[512,2048]{1,0:T(8,128)(2,1)}) %all-gather.11.cloned.1.call-update) | async-done | bytes 2097168 | tf_op jit(solution)/shard_map/all_gather | solution.py:24
  154.2 3.8 fusion
  158.1 4.0 fusion.1
  162.1 6.2 pad_maximum_fusion
  168.3 10.1 %copy.17 = bf16[2048,1792]{1,0:T(8,128)(2,1)} copy(bf16[2048,1792]{0,1:T(8,128)(2,1)} %pad_maximum_fusion) | data formatting | bytes 14680064
  178.4 0.9 copy-done
  179.3 2.4 stack.2
  181.8 10.5 %all-to-all-start = ((bf16[32,64,896]{2,1,0:T(8,128)(2,1)}), bf16[32,64,896]{2,1,0:T(8,128)(2,1)}, u32[]{:S(2)}, u32[]{:S(2)}) async-start(bf16[32,64,896]{2,1,0:T(8,128)(2,1)} %stack.2), calls=%async_computation | async-start | bytes 7340032 | tf_op jit(solution)/shard_map/all_to_all | solution.py:10
  192.3 5.3 fusion.2
  197.6 6.1 copy.19
  204.0 88.0 %all-to-all-done = bf16[32,64,896]{2,1,0:T(8,128)(2,1)} async-done(((bf16[32,64,896]{2,1,0:T(8,128)(2,1)}), bf16[32,64,896]{2,1,0:T(8,128)(2,1)}, u32[]{:S(2)}, u32[]{:S(2)}) %all-to-all-start) | async-done | bytes 3670048 | tf_op jit(solution)/shard_map/all_to_all | solution.py:10
  292.0 6.7 fusion.14
  298.6 7.7 add_convert_fusion
  306.4 202.1 %reduce-scatter.10.cloned.1.call-done = bf16[64,1792]{1,0:T(8,128)(2,1)} async-done(((bf16[2048,1792]{1,0:T(8,128)(2,1)}), bf16[64,1792]{1,0:T(8,128)(2,1)}) %reduce-scatter.10.cloned.1.call-update) | async-done | bytes 229392
  508.5 1.7 fusion.13
  510.2 222.8 %reduce-scatter.12.cloned.1.call-done = bf16[64,896]{1,0:T(8,128)(2,1)} async-done(((bf16[2048,896]{1,0:T(8,128)(2,1)}), bf16[64,896]{1,0:T(8,128)(2,1)}) %reduce-scatter.12.cloned.1.call-update) | async-done | bytes 114704
  733.0 38.7 %reduce-scatter.8.cloned.1.call-done = bf16[512,256]{1,0:T(8,128)(2,1)} async-done(((bf16[512,2048]{1,0:T(8,128)(2,1)}), bf16[512,256]{1,0:T(8,128)(2,1)}) %reduce-scatter.8.cloned.1.call-update) | async-done | bytes 262160 | tf_op jit(solution)/shard_map/reduce_scatter | solution.py:52
  (28 shorter events, 0.5 us)
Async XLA Ops:
  7.2 34.8 %all-gather.5.cloned.1.call-start = ((), (), s32[]{:S(2)}) async-start(), calls=%async_computation.4 | async-start | bytes 2359296 | tf_op jit(solution)/shard_map/all_gather | solution.py:25
  7.9 117.1 %all-gather.7.cloned.1.call-start = ((), (), s32[]{:S(2)}) async-start(), calls=%async_computation.5 | async-start | bytes 3784704 | tf_op jit(solution)/shard_map/all_gather | solution.py:29
  8.6 145.6 %all-gather.11.cloned.1.call-start = ((), (), s32[]{:S(2)}) async-start(), calls=%async_computation.8 | async-start | bytes 2359296 | tf_op jit(solution)/shard_map/all_gather | solution.py:24
  9.4 289.3 %all-gather.9.cloned.1.call-start = ((), (), s32[]{:S(2)}) async-start(), calls=%async_computation.6 | async-start | bytes 3784704 | tf_op jit(solution)/shard_map/all_gather | solution.py:50
  10.0 498.6 %reduce-scatter.10.cloned.1.call-start = ((), (), s32[]{:S(2)}) async-start(), calls=%async_computation.9 | async-start | bytes 7569408
  132.0 26.1 %copy-start.6 = (bf16[512,896]{1,0:T(8,128)(2,1)}, bf16[512,896]{1,0:T(8,128)(2,1)S(1)}, u32[]{:S(2)}) copy-start(bf16[512,896]{1,0:T(8,128)(2,1)S(1)} %get-tuple-element.14) | copy-start | bytes 2752516
  154.2 3.9 copy-start.2
  154.2 3.9 copy-start.4
  154.2 3.9 copy-start.8
  178.4 0.9 copy-start
  181.8 10.5 %copy-start.1 = (bf16[512,2048]{1,0:T(8,128)(2,1)S(1)}, bf16[512,2048]{1,0:T(8,128)(2,1)}, u32[]{:S(2)}) copy-start(bf16[512,2048]{1,0:T(8,128)(2,1)} %all-gather.5.cloned.1.call-done) | copy-start | bytes 6291460
  181.8 10.5 %copy-start.3 = (bf16[512,896]{1,0:T(8,128)(2,1)S(1)}, bf16[512,896]{1,0:T(8,128)(2,1)}, u32[]{:S(2)}) copy-start(bf16[512,896]{1,0:T(8,128)(2,1)} %param.10) | copy-start | bytes 2752516
  181.8 110.2 %all-to-all-start = ((bf16[32,64,896]{2,1,0:T(8,128)(2,1)}), bf16[32,64,896]{2,1,0:T(8,128)(2,1)}, u32[]{:S(2)}, u32[]{:S(2)}) async-start(bf16[32,64,896]{2,1,0:T(8,128)(2,1)} %stack.2), calls=%async_computation | async-start | bytes 7340032 | tf_op jit(solution)/shard_map/all_to_all | solution.py:10
  192.2 540.8 %reduce-scatter.12.cloned.1.call-start = ((), (), s32[]{:S(2)}) async-start(), calls=%async_computation.10 | async-start | bytes 3784704
  203.7 88.2 %copy-start.7 = (bf16[512,896]{1,0:T(8,128)(2,1)S(1)}, bf16[512,896]{1,0:T(8,128)(2,1)}, u32[]{:S(2)}) copy-start(bf16[512,896]{1,0:T(8,128)(2,1)} %copy-done.6) | copy-start | bytes 2752516
  203.7 567.9 %reduce-scatter.8.cloned.1.call-start = ((), (), s32[]{:S(2)}) async-start(), calls=%async_computation.7 | async-start | bytes 2359296 | tf_op jit(solution)/shard_map/reduce_scatter | solution.py:52
  291.9 6.7 copy-start.5
Sparse Core Ops, SparseCore 0:
  9.8 32.1 all-gather.4
  44.6 80.3 all-gather.6
  126.8 27.3 all-gather.10
  156.6 124.7 all-gather.8
  285.4 223.1 reduce-scatter.9
  512.8 220.0 reduce-scatter.11
  736.1 35.4 reduce-scatter.7
